TPU v7x, 32 devices: a whole 2x2x4 slice. The times are simulated.
32 devices in a mesh: grp: 2 (over x), inp: 4 (over y, core), out: 4 (over z).
Axes of the slice: x: 2, y: 2, z: 4, core: 2. Of those that a mesh axis runs over, the one named last changes fastest.
Arguments:
- activations: bfloat16 [4, 512, 8192], P('grp', 'out', 'inp'), parts along dimension 0, may hold values from -6 to 6
- out_grads: bfloat16 [4, 512, 28672], P('grp', 'inp', 'out'), parts along dimension 0, may hold values from -6 to 6
- query_grads: bfloat16 [2, 28672, 8192], P(None, 'out', 'inp'), may hold values from -0.00036621094 to 0.00036621094
- token_ids: int32 [4, 512], P('grp'), parts along dimension 0, may hold values from 0 to 128255
- loss_mask: int32 [4, 512], P('grp'), parts along dimension 0, may hold values 0 or 1
Outputs:
- scores: float32 [2, 4, 512], P(None, 'grp'), parts along dimension 1
There are 2 independent parts, one for each index of `grp`. A program takes and returns all parts, laid end to end along the dimension named above; an argument that names none is the same for every part. Nothing has to cross between parts.
All inputs are finite; a program needn't handle non-finite values.
Results may differ from a plain program's by a relative error of at most 0.0003.
Values may be sent and summed in bfloat16 or wider, within the bound.
A program may use at most 128 MiB of HBM per device.

v0:
```python
import jax
import jax.numpy as jnp
from jax import lax
from jax.sharding import PartitionSpec as P


def shards(activations, out_grads, query_grads, token_ids, loss_mask):
    blocks = activations.shape[0]
    partials = []
    for number in range(blocks):
        gathered = lax.all_gather(activations[number], "out", axis=0, tiled=True)
        projected = jnp.einsum(
            "to,qoi->tqi",
            lax.all_gather(out_grads[number], "inp", axis=0, tiled=True),
            query_grads,
            preferred_element_type=jnp.float32,
        )
        partial_value = jnp.sum(projected * gathered.astype(jnp.float32)[:, None, :], axis=2)
        partial_value = lax.psum(partial_value, ("inp", "out"))
        partials.append(partial_value)
    stacked = jnp.stack(partials)
    equal = token_ids[:, :, None] == token_ids[:, None, :]
    counts = jnp.sum(equal.astype(jnp.int32), axis=2)
    weight = loss_mask.astype(jnp.float32) / counts.astype(jnp.float32)
    return jnp.transpose(stacked * weight[:, :, None], (2, 0, 1))


def solution(mesh):
    in_specs = (
        P("grp", "out", "inp"),
        P("grp", "inp", "out"),
        P(None, "out", "inp"),
        P("grp", None),
        P("grp", None),
    )
    out_specs = P(None, "grp", None)
    return jax.shard_map(shards, mesh=mesh, in_specs=in_specs, out_specs=out_specs, check_vma=False)
```

profile of v0, /device:TPU:0, one launch (start us, length us, event | category | flops | bytes accessed | tf_op | source)
XLA Modules:
  0.0 289.7 jit_solution(5545557528172188764)
XLA Ops:
  6.5 0.0 copy-start
  6.5 0.0 copy-start.1
  6.5 0.0 all-gather.15.cloned.1.call-start
  6.5 2.3 fusion.10
  8.9 0.0 all-gather.15.cloned.1.call-update
  8.9 0.0 all-gather.11.cloned.1.call-start
  8.9 0.7 all-gather.11.cloned.1.call-update
  9.6 0.0 all-gather.13.cloned.1.call-start
  9.7 4.1 %fusion.9 = (bf16[1,128,7168]{2,1,0:T(8,128)(2,1)}, bf16[1,128,7168]{2,1,0:T(8,128)(2,1)}) fusion(bf16[2,128,7168]{2,1,0:T(8,128)(2,1)} %param.6), kind=kLoop, calls=%fused_computation.12 | loop fusion | bytes 7340032 | tf_op jit(solution)/shard_map/slice | solution.py:14
  13.8 0.0 all-gather.13.cloned.1.call-update
  13.8 0.0 all-gather.9.cloned.1.call-start
  13.9 0.5 all-gather.9.cloned.1.call-update
  14.4 0.0 copy-done
  14.4 0.4 convert_reduce_fusion
  14.8 0.0 copy-done.1
  14.8 42.6 %all-gather.15.cloned.1.call-done = bf16[1,512,2048]{2,1,0:T(8,128)(2,1)} async-done(((bf16[1,128,2048]{2,1,0:T(8,128)(2,1)}), bf16[1,512,2048]{2,1,0:T(8,128)(2,1)}) %all-gather.15.cloned.1.call-update) | async-done | bytes 2097168 | tf_op jit(solution)/shard_map/all_gather | solution.py:11
  57.4 4.1 %bitcast_convert_fusion = f32[512,2048]{1,0:T(8,128)} fusion(bf16[1,512,2048]{2,1,0:T(8,128)(2,1)} %all-gather.15.cloned.1.call-done), kind=kLoop, calls=%fused_computation.6 | loop fusion | flops 1048576 | bytes 6291456 | tf_op jit(solution)/shard_map/convert_element_type | solution.py:18
  61.5 42.0 %all-gather.11.cloned.1.call-done = bf16[1,512,2048]{2,1,0:T(8,128)(2,1)} async-done(((bf16[1,128,2048]{2,1,0:T(8,128)(2,1)}), bf16[1,512,2048]{2,1,0:T(8,128)(2,1)}) %all-gather.11.cloned.1.call-update) | async-done | bytes 2097168 | tf_op jit(solution)/shard_map/all_gather | solution.py:11
  103.5 4.1 %bitcast_convert_fusion.1 = f32[512,2048]{1,0:T(8,128)} fusion(bf16[1,512,2048]{2,1,0:T(8,128)(2,1)} %all-gather.11.cloned.1.call-done), kind=kLoop, calls=%fused_computation.7 | loop fusion | flops 1048576 | bytes 6291456 | tf_op jit(solution)/shard_map/convert_element_type | solution.py:18
  107.6 48.6 %all-gather.13.cloned.1.call-done = bf16[1,512,7168]{2,1,0:T(8,128)(2,1)} async-done(((bf16[1,128,7168]{2,1,0:T(8,128)(2,1)}), bf16[1,512,7168]{2,1,0:T(8,128)(2,1)}) %all-gather.13.cloned.1.call-update) | async-done | bytes 7340048 | tf_op jit(solution)/shard_map/all_gather | solution.py:14
  156.2 39.0 %multiply_reduce_fusion = f32[512,2]{0,1:T(2,128)S(1)} fusion(f32[512,2048]{1,0:T(8,128)} %bitcast_convert_fusion, bf16[2,7168,2048]{2,1,0:T(8,128)(2,1)} %param.7, bf16[1,512,7168]{2,1,0:T(8,128)(2,1)} %all-gather.13.cloned.1.call-done), kind=kOutput, calls=%fused_computation | convolution fusion | flops 30068965376 | bytes 70258688 | tf_op jit(solution)/shard_map/to,qoi->tqi/dot_general | solution.py:12
  195.2 14.8 %all-gather.9.cloned.1.call-done = bf16[1,512,7168]{2,1,0:T(8,128)(2,1)} async-done(((bf16[1,128,7168]{2,1,0:T(8,128)(2,1)}), bf16[1,512,7168]{2,1,0:T(8,128)(2,1)}) %all-gather.9.cloned.1.call-update) | async-done | bytes 7340048 | tf_op jit(solution)/shard_map/all_gather | solution.py:14
  210.0 38.8 %multiply_reduce_fusion.1 = f32[512,2]{0,1:T(2,128)S(1)} fusion(f32[512,2048]{1,0:T(8,128)} %bitcast_convert_fusion.1, bf16[2,7168,2048]{2,1,0:T(8,128)(2,1)} %param.7, bf16[1,512,7168]{2,1,0:T(8,128)(2,1)} %all-gather.9.cloned.1.call-done), kind=kOutput, calls=%fused_computation.1 | convolution fusion | flops 30068965376 | bytes 70258688 | tf_op jit(solution)/shard_map/to,qoi->tqi/dot_general | solution.py:12
  248.8 33.8 %all-reduce = (f32[1,512,2]{1,0,2:T(1,128)S(1)}, f32[1,512,2]{1,0,2:T(1,128)S(1)}) all-reduce(f32[1,512,2]{1,0,2:T(1,128)S(1)} %stack.10, f32[1,512,2]{1,0,2:T(1,128)S(1)} %stack.9), channel_id=1, replica_groups=mesh['grp'=2,'inp'=4,'out'=4] {'inp','out'}, use_global_device_ids=true, to_apply=%region_3.0 | all-reduce | flops 2048 | bytes 16384 | tf_op jit(solution)/shard_map/psum | solution.py:19
  282.6 0.6 fusion.8
  (3 shorter events, 0.0 us)
Async XLA Ops:
  6.5 7.9 %copy-start = (s32[2,512]{1,0:T(2,128)S(1)}, s32[2,512]{1,0:T(2,128)}, u32[]{:S(2)}) copy-start(s32[2,512]{1,0:T(2,128)} %param.8) | copy-start | bytes 12292
  6.5 8.3 %copy-start.1 = (s32[2,512]{1,0:T(2,128)S(1)}, s32[2,512]{1,0:T(2,128)}, u32[]{:S(2)}) copy-start(s32[2,512]{1,0:T(2,128)} %param.9) | copy-start | bytes 12292
  6.5 50.9 %all-gather.15.cloned.1.call-start = ((), (), s32[]{:S(2)}) async-start(), calls=%async_computation.3 | async-start | bytes 2621440 | tf_op jit(solution)/shard_map/all_gather | solution.py:11
  8.9 94.6 %all-gather.11.cloned.1.call-start = ((), (), s32[]{:S(2)}) async-start(), calls=%async_computation.1 | async-start | bytes 2621440 | tf_op jit(solution)/shard_map/all_gather | solution.py:11
  9.6 146.6 %all-gather.13.cloned.1.call-start = ((), (), s32[]{:S(2)}) async-start(), calls=%async_computation.2 | async-start | bytes 9175040 | tf_op jit(solution)/shard_map/all_gather | solution.py:14
  13.8 196.1 %all-gather.9.cloned.1.call-start = ((), (), s32[]{:S(2)}) async-start(), calls=%async_computation | async-start | bytes 9175040 | tf_op jit(solution)/shard_map/all_gather | solution.py:14
Sparse Core Ops, SparseCore 0:
  9.0 48.3 all-gather.14
  59.0 44.4 all-gather.10
  105.0 51.1 all-gather.12
  157.6 52.2 all-gather.8
where the time goes:
time: 290 us
  waiting for transfers between devices  149 us (51%)
  matrix products  77.8 us (27%)
  blocking collectives  33.8 us (12%)
  between operations  13.2 us (5%)
  other arithmetic  9.25 us (3%)
  local copies, waits for them, and re-layouts  6.45 us (2%)
    all_gather x2, waiting for transfers between devices, shards(): gathered = lax.all_gather(activations[number], 'out', axis=0, tiled=True)  84.5 us
    dot_general x2, matrix products, shards(): jnp.einsum('to,qoi->tqi', lax.all_gather(out_grads[number], 'inp', axis=0...  77.8 us
    all_gather x2, waiting for transfers between devices, shards(): lax.all_gather(out_grads[number], 'inp', axis=0, tiled=True)  63.4 us
    psum x1, blocking collectives, shards(): partial_value = lax.psum(partial_value, ('inp', 'out'))  33.8 us
    convert_element_type x2, other arithmetic, shards(): gathered.astype(jnp.float32)[:, None, :]  8.22 us
  transfers between devices with their start and end apart: 4, of which 4 were waited for; matrix products, arithmetic and copies ran while one was open for 18% of the time, Pallas kernels for 0%

commit v1 on v0

--- a/solution.py
+++ b/solution.py
@@ -2,6 +2,16 @@
 import jax.numpy as jnp
 from jax import lax
 from jax.sharding import PartitionSpec as P
+
+
+def refer_the_meshes(local_x, array_dim):
+    local_x = jnp.moveaxis(local_x, 0, array_dim)
+    left_arr = local_x.shape
+    return local_x.reshape(
+        *left_arr[:array_dim],
+        left_arr[array_dim] * left_arr[array_dim + 1],
+        *left_arr[array_dim + 2 :]
+    )
 
 
 def shards(activations, out_grads, query_grads, token_ids, loss_mask):
@@ -9,11 +19,40 @@
     partials = []
     for number in range(blocks):
         gathered = lax.all_gather(activations[number], "out", axis=0, tiled=True)
-        projected = jnp.einsum(
-            "to,qoi->tqi",
-            lax.all_gather(out_grads[number], "inp", axis=0, tiled=True),
-            query_grads,
-            preferred_element_type=jnp.float32,
+
+        def strings_raise(point, peer_axis, k_dim, field_in, dim_no):
+            before = lax.axis_size(peer_axis)
+            piece_out = lax.axis_index(peer_axis)
+            ready, o_now, mat_out = (before, piece_out, point.shape[k_dim])
+            samples = tuple(((pp, (pp + 1) % ready) for pp in range(ready)))
+            pile = tuple(((pp, (pp - 1) % ready) for pp in range(ready)))
+            known = ready // 2
+            lower = {}
+            z_new = block_next = point
+            for w in tuple(range(known + 1)):
+                field_out = lax.ppermute(z_new, peer_axis, perm=samples) if w < known else None
+                y2 = (
+                    lax.ppermute(block_next, axis_name=peer_axis, perm=pile)
+                    if w < ready - known - 1
+                    else None
+                )
+                lower[-w] = field_in(z_new, (o_now - w) % ready * mat_out)
+                if 0 < w < ready - known:
+                    lower[w] = field_in(block_next, (o_now + w) % ready * mat_out)
+                z_new, block_next = (field_out, y2)
+            r_now = tuple((lower[rr] for rr in sorted(lower)))
+            lower = jnp.stack(r_now, 0)
+            lower = lower[(jnp.arange(ready) - o_now + known) % ready]
+            return refer_the_meshes(lower, dim_no)
+
+        projected = strings_raise(
+            out_grads[number],
+            peer_axis="inp",
+            k_dim=0,
+            field_in=lambda shard, offset: jnp.einsum(
+                "to,qoi->tqi", shard, query_grads, preferred_element_type=jnp.float32
+            ),
+            dim_no=0,
         )
         partial_value = jnp.sum(projected * gathered.astype(jnp.float32)[:, None, :], axis=2)
         partial_value = lax.psum(partial_value, ("inp", "out"))

time: 290 us -> 294 us (1.014)
  waiting for transfers between devices: 149 us -> 6.61 us
  matrix products: 77.8 us -> 181 us
  local copies, waits for them, and re-layouts: 6.45 us -> 25.3 us
  other arithmetic: 9.25 us -> 25 us
  starting transfers between devices: 0.12 us -> 7.4 us
    dot_general x2 -> x8, matrix products: 77.8 us -> 181 us  [shards(): jnp.einsum('to,qoi->tqi', shard, query_grads, preferred_element_type=jnp....]
    all_gather x2, waiting for transfers between devices: 84.5 us -> 0.01 us  [shards(): gathered = lax.all_gather(activations[number], 'out', axis=0, tiled=True)]
    all_gather x2 -> x0, waiting for transfers between devices: 63.4 us -> none  [shards(): lax.all_gather(out_grads[number], 'inp', axis=0, tiled=True)]
    gather x0 -> x2, local copies, waits for them, and re-layouts: none -> 15.4 us  [strings_raise(): lower = lower[(jnp.arange(ready) - o_now + known) % ready]]
    another operation x0 -> x2, other arithmetic: none -> 9.8 us  [strings_raise(): lower = jnp.stack(r_now, 0)]
    convert_element_type x2 -> x0, other arithmetic: 8.22 us -> none  [shards(): gathered.astype(jnp.float32)[:, None, :]]
    mul x0 -> x2, other arithmetic: none -> 8.13 us  [shards(): projected * gathered.astype(jnp.float32)[:, None, :]]
    ppermute x0 -> x6, starting transfers between devices: none -> 7.36 us  [the longest x4 4.35 us: strings_raise(): lax.ppermute(z_new, peer_axis, perm=samples)]
  transfers between devices with their start and end apart: 4 -> 8, of which waited for: 4 -> 1; matrix products, arithmetic and copies ran while one was open for 18% -> 63% of each run, Pallas kernels for 0% -> 0%
where the time goes in v1:
time: 294 us; the launch traced here: 293 us
  matrix products  181 us (62%)
  blocking collectives  34.2 us (12%)
  local copies, waits for them, and re-layouts  25.3 us (9%)
  other arithmetic  25 us (9%)
  between operations  13.5 us (5%)
  starting transfers between devices  7.4 us (3%)
  waiting for transfers between devices  6.61 us (2%)
    dot_general x8, matrix products, shards(): jnp.einsum('to,qoi->tqi', shard, query_grads, preferred_element_type=jnp....  181 us
    psum x1, blocking collectives, shards(): partial_value = lax.psum(partial_value, ('inp', 'out'))  34.2 us
    gather x2, local copies, waits for them, and re-layouts, strings_raise(): lower = lower[(jnp.arange(ready) - o_now + known) % ready]  15.4 us
    another operation x2, other arithmetic, strings_raise(): lower = jnp.stack(r_now, 0)  9.8 us
    mul x2, other arithmetic, shards(): projected * gathered.astype(jnp.float32)[:, None, :]  8.13 us
    ppermute x4, waiting for transfers between devices, strings_raise(): lax.ppermute(z_new, peer_axis, perm=samples)  6.57 us
    reduce_sum x2, other arithmetic, shards(): jnp.sum(projected * gathered.astype(jnp.float32)[:, None, :], axis=2)  5.99 us
  transfers between devices with their start and end apart: 8, of which 1 were waited for; matrix products, arithmetic and copies ran while one was open for 63% of the time, Pallas kernels for 0%

profile of v1, /device:TPU:0, one launch (start us, length us, event | category | flops | bytes accessed | tf_op | source)
XLA Modules:
  0.0 293.4 jit_solution(6443480257032775068)
XLA Ops:
  6.5 0.0 all-gather.5.cloned.1.call-start
  6.5 2.3 fusion.13
  8.8 0.0 all-gather.5.cloned.1.call-update
  8.9 0.0 all-gather.7.cloned.1.call-start
  8.9 4.2 %slice_bitcast_fusion.1 = (bf16[128,7168]{1,0:T(8,128)(2,1)}, bf16[128,7168]{1,0:T(8,128)(2,1)}) fusion(bf16[2,128,7168]{2,1,0:T(8,128)(2,1)} %param.6), kind=kLoop, calls=%fused_computation.26 | loop fusion | bytes 7340032 | tf_op jit(solution)/shard_map/squeeze | solution.py:49
  13.1 0.5 collective-permute-start
  13.6 1.9 collective-permute-start.2
  15.5 0.7 collective-permute-start.3
  16.2 1.1 collective-permute-start.5
  17.3 0.0 all-gather.7.cloned.1.call-update
  17.3 0.0 copy-start.8
  17.3 0.0 copy-start.9
  17.3 21.3 %convolution_bitcast_fusion.5 = f32[1,128,2,2048]{3,1,2,0:T(8,128)S(1)} fusion(bf16[2,7168,2048]{2,1,0:T(8,128)(2,1)} %param.7, bf16[2,128,7168]{2,1,0:T(8,128)(2,1)} %param.6), kind=kOutput, calls=%fused_computation.11 | convolution fusion | flops 7516192768 | bytes 62652416 | tf_op jit(solution)/shard_map/to,qoi->tqi/dot_general | solution.py:52
  38.6 0.0 copy-done.8
  38.6 0.4 convert_reduce_fusion
  39.0 0.0 copy-done.9
  39.0 0.6 convert_divide_fusion
  39.7 22.8 %convolution_bitcast_fusion.1 = f32[1,128,2,2048]{3,1,2,0:T(8,128)} fusion(bf16[2,7168,2048]{2,1,0:T(8,128)(2,1)} %param.7, bf16[2,128,7168]{2,1,0:T(8,128)(2,1)} %param.6), kind=kOutput, calls=%fused_computation.7 | convolution fusion | flops 7516192768 | bytes 62652416 | tf_op jit(solution)/shard_map/to,qoi->tqi/dot_general | solution.py:52
  62.5 0.0 collective-permute-done
  62.5 0.7 collective-permute-start.1
  63.1 23.4 %convolution_bitcast_fusion.6 = f32[1,128,2,2048]{3,1,2,0:T(8,128)} fusion(bf16[2,7168,2048]{2,1,0:T(8,128)(2,1)} %param.7, bf16[128,7168]{1,0:T(8,128)(2,1)} %collective-permute-done), kind=kOutput, calls=%fused_computation.12 | convolution fusion | flops 7516192768 | bytes 62652416 | tf_op jit(solution)/shard_map/to,qoi->tqi/dot_general | solution.py:52
  86.6 6.6 %collective-permute-done.3 = bf16[128,7168]{1,0:T(8,128)(2,1)} collective-permute-done((bf16[128,7168]{1,0:T(8,128)(2,1)}, bf16[128,7168]{1,0:T(8,128)(2,1)}, u32[]{:S(2)}, u32[]{:S(2)}) %collective-permute-start.3) | collective-permute-done | bytes 1835040 | tf_op jit(solution)/shard_map/ppermute | solution.py:33
  93.1 2.5 collective-permute-start.4
  95.6 22.7 %convolution_bitcast_fusion.2 = f32[1,128,2,2048]{3,1,2,0:T(8,128)} fusion(bf16[2,7168,2048]{2,1,0:T(8,128)(2,1)} %param.7, bf16[128,7168]{1,0:T(8,128)(2,1)} %collective-permute-done.3), kind=kOutput, calls=%fused_computation.8 | convolution fusion | flops 7516192768 | bytes 62652416 | tf_op jit(solution)/shard_map/to,qoi->tqi/dot_general | solution.py:52
  118.3 0.0 collective-permute-done.2
  118.3 22.7 %convolution_bitcast_fusion.4 = f32[1,128,2,2048]{3,1,2,0:T(8,128)} fusion(bf16[2,7168,2048]{2,1,0:T(8,128)(2,1)} %param.7, bf16[128,7168]{1,0:T(8,128)(2,1)} %collective-permute-done.2), kind=kOutput, calls=%fused_computation.10 | convolution fusion | flops 7516192768 | bytes 62652416 | tf_op jit(solution)/shard_map/to,qoi->tqi/dot_general | solution.py:52
  141.1 0.0 collective-permute-done.5
  141.1 22.7 %convolution_bitcast_fusion = f32[1,128,2,2048]{3,1,2,0:T(8,128)} fusion(bf16[2,7168,2048]{2,1,0:T(8,128)(2,1)} %param.7, bf16[128,7168]{1,0:T(8,128)(2,1)} %collective-permute-done.5), kind=kOutput, calls=%fused_computation.6 | convolution fusion | flops 7516192768 | bytes 62652416 | tf_op jit(solution)/shard_map/to,qoi->tqi/dot_general | solution.py:52
  163.8 0.0 all-gather.5.cloned.1.call-done
  163.8 4.0 %convert.2 = f32[4,128,2048]{2,1,0:T(8,128)} convert(bf16[4,128,2048]{2,1,0:T(8,128)(2,1)} %bitcast.62) | non-fusion elementwise | flops 1048576 | bytes 6291456 | tf_op jit(solution)/shard_map/mul | solution.py:57
  167.8 0.0 all-gather.7.cloned.1.call-done
  167.8 4.1 %convert.3 = f32[4,128,2048]{2,1,0:T(8,128)} convert(bf16[4,128,2048]{2,1,0:T(8,128)(2,1)} %bitcast.63) | non-fusion elementwise | flops 1048576 | bytes 6291456 | tf_op jit(solution)/shard_map/mul | solution.py:57
  171.9 0.0 copy-start.4
  171.9 0.0 copy-start.6
  171.9 0.0 collective-permute-done.1
  171.9 22.9 %convolution_bitcast_fusion.7 = f32[1,128,2,2048]{3,1,2,0:T(8,128)} fusion(bf16[2,7168,2048]{2,1,0:T(8,128)(2,1)} %param.7, bf16[128,7168]{1,0:T(8,128)(2,1)} %collective-permute-done.1), kind=kOutput, calls=%fused_computation.13 | convolution fusion | flops 7516192768 | bytes 62652416 | tf_op jit(solution)/shard_map/to,qoi->tqi/dot_general | solution.py:52
  194.8 0.0 copy-done.4
  194.8 0.0 copy-done.6
  194.8 5.0 %pad_maximum_fusion = f32[4,128,2,2048]{3,1,2,0:T(8,128)} fusion(f32[1,128,2,2048]{3,1,2,0:T(8,128)S(1)} %copy-done.6, f32[1,128,2,2048]{3,1,2,0:T(8,128)S(1)} %convolution_bitcast_fusion.5, f32[1,128,2,2048]{3,1,2,0:T(8,128)S(1)} %copy-done.4, f32[1,128,2,2048]{3,1,2,0:T(8,128)} %convolution_bitcast_fusion.7), kind=kLoop, calls=%fused_computation.2 | loop fusion | flops 6291456 | bytes 16777216 | tf_op jit(solution)/shard_map/stack | solution.py:44
  199.8 7.7 %gather_fusion = f32[4,128,2,2048]{3,1,2,0:T(8,128)} fusion(f32[4,128,2,2048]{3,1,2,0:T(8,128)} %pad_maximum_fusion, s32[1024]{0:T(1024)S(1)} %pad_clamp_fusion), kind=kCustom, calls=%fused_computation | custom fusion | bytes 16777232 | tf_op jit(solution)/shard_map/gather | solution.py:45
  207.5 0.0 copy-start.2
  207.5 0.0 copy-start.3
  207.5 0.0 copy-start.5
  207.5 0.0 collective-permute-done.4
  207.5 22.9 %convolution_bitcast_fusion.3 = f32[1,128,2,2048]{3,1,2,0:T(8,128)} fusion(bf16[2,7168,2048]{2,1,0:T(8,128)(2,1)} %param.7, bf16[128,7168]{1,0:T(8,128)(2,1)} %collective-permute-done.4), kind=kOutput, calls=%fused_computation.9 | convolution fusion | flops 7516192768 | bytes 62652416 | tf_op jit(solution)/shard_map/to,qoi->tqi/dot_general | solution.py:52
  230.4 0.0 copy-done.2
  230.4 0.0 copy-done.3
  230.4 0.0 copy-done.5
  230.4 4.8 %pad_maximum_fusion.1 = f32[4,128,2,2048]{3,1,2,0:T(8,128)} fusion(f32[1,128,2,2048]{3,1,2,0:T(8,128)S(1)} %copy-done.5, f32[1,128,2,2048]{3,1,2,0:T(8,128)S(1)} %copy-done.2, f32[1,128,2,2048]{3,1,2,0:T(8,128)S(1)} %copy-done.3, f32[1,128,2,2048]{3,1,2,0:T(8,128)} %convolution_bitcast_fusion.3), kind=kLoop, calls=%fused_computation.3 | loop fusion | flops 6291456 | bytes 16777216 | tf_op jit(solution)/shard_map/stack | solution.py:44
  235.2 7.7 %gather_fusion.1 = f32[4,128,2,2048]{3,1,2,0:T(8,128)} fusion(f32[4,128,2,2048]{3,1,2,0:T(8,128)} %pad_maximum_fusion.1, s32[1024]{0:T(1024)S(1)} %pad_clamp_fusion), kind=kCustom, calls=%fused_computation.1 | custom fusion | bytes 16777232 | tf_op jit(solution)/shard_map/gather | solution.py:45
  242.9 0.0 copy-start
  242.9 0.0 copy-start.1
  242.9 5.4 %multiply_reduce_fusion.1 = f32[4,128,2]{1,2,0:T(2,128)S(1)} fusion(f32[4,128,2,2048]{3,1,2,0:T(8,128)} %gather_fusion, f32[4,128,2048]{2,1,0:T(8,128)} %convert.2), kind=kLoop, calls=%fused_computation.5 | loop fusion | flops 4193280 | bytes 12587008 | tf_op jit(solution)/shard_map/reduce_sum | solution.py:57
  248.3 1.6 copy-done
  249.9 1.2 copy-done.1
  251.1 0.0 copy-start.7
  251.1 0.6 multiply_reduce_fusion
  251.7 34.2 %all-reduce = (f32[1,512,2]{1,2,0:T(2,128)S(1)}, f32[1,512,2]{1,2,0:T(2,128)S(1)}) all-reduce(f32[1,512,2]{1,2,0:T(2,128)S(1)} %bitcast.65, f32[1,512,2]{1,2,0:T(2,128)S(1)} %bitcast.64), channel_id=1, replica_groups=mesh['grp'=2,'inp'=4,'out'=4] {'inp','out'}, use_global_device_ids=true, to_apply=%region_3.4 | all-reduce | flops 2048 | bytes 16384 | tf_op jit(solution)/shard_map/psum | solution.py:58
  285.9 0.0 copy-done.7
  285.9 0.6 copy.7
  (3 shorter events, 0.0 us)
Async XLA Ops:
  6.5 157.3 %all-gather.5.cloned.1.call-start = ((), (), s32[]{:S(2)}) async-start(), calls=%async_computation | async-start | bytes 2621440 | tf_op jit(solution)/shard_map/all_gather | solution.py:21
  8.9 159.0 %all-gather.7.cloned.1.call-start = ((), (), s32[]{:S(2)}) async-start(), calls=%async_computation.1 | async-start | bytes 2621440 | tf_op jit(solution)/shard_map/all_gather | solution.py:21
  13.1 49.4 %collective-permute-start = (bf16[128,7168]{1,0:T(8,128)(2,1)}, bf16[128,7168]{1,0:T(8,128)(2,1)}, u32[]{:S(2)}, u32[]{:S(2)}) collective-permute-start(bf16[128,7168]{1,0:T(8,128)(2,1)} %get-tuple-element.7), channel_id=1, source_target_pairs={{0,4},{4,8},{8,12},{12,0},{1,5},{5,9},{9,13},{13,1},{2,6},{6,10},{... | collective-permute-start | bytes 5505032 | tf_op jit(solution)/shard_map/ppermute | solution.py:33
  13.6 104.8 %collective-permute-start.2 = (bf16[128,7168]{1,0:T(8,128)(2,1)}, bf16[128,7168]{1,0:T(8,128)(2,1)}, u32[]{:S(2)}, u32[]{:S(2)}) collective-permute-start(bf16[128,7168]{1,0:T(8,128)(2,1)} %get-tuple-element.7), channel_id=1, source_target_pairs={{0,12},{4,0},{8,4},{12,8},{1,13},{5,1},{9,5},{13,9},{2,14},{6,2},{... | collective-permute-start | bytes 5505032 | tf_op jit(solution)/shard_map/ppermute | solution.py:35
  15.5 77.6 %collective-permute-start.3 = (bf16[128,7168]{1,0:T(8,128)(2,1)}, bf16[128,7168]{1,0:T(8,128)(2,1)}, u32[]{:S(2)}, u32[]{:S(2)}) collective-permute-start(bf16[128,7168]{1,0:T(8,128)(2,1)} %get-tuple-element.8), channel_id=1, source_target_pairs={{0,4},{4,8},{8,12},{12,0},{1,5},{5,9},{9,13},{13,1},{2,6},{6,10},{... | collective-permute-start | bytes 5505032 | tf_op jit(solution)/shard_map/ppermute | solution.py:33
  16.2 124.9 %collective-permute-start.5 = (bf16[128,7168]{1,0:T(8,128)(2,1)}, bf16[128,7168]{1,0:T(8,128)(2,1)}, u32[]{:S(2)}, u32[]{:S(2)}) collective-permute-start(bf16[128,7168]{1,0:T(8,128)(2,1)} %get-tuple-element.8), channel_id=1, source_target_pairs={{0,12},{4,0},{8,4},{12,8},{1,13},{5,1},{9,5},{13,9},{2,14},{6,2},{... | collective-permute-start | bytes 5505032 | tf_op jit(solution)/shard_map/ppermute | solution.py:35
  17.3 21.3 %copy-start.8 = (s32[2,512]{1,0:T(2,128)S(1)}, s32[2,512]{1,0:T(2,128)}, u32[]{:S(2)}) copy-start(s32[2,512]{1,0:T(2,128)} %param.8) | copy-start | bytes 12292
  17.3 21.7 %copy-start.9 = (s32[2,512]{1,0:T(2,128)S(1)}, s32[2,512]{1,0:T(2,128)}, u32[]{:S(2)}) copy-start(s32[2,512]{1,0:T(2,128)} %param.9) | copy-start | bytes 12292
  62.5 109.5 %collective-permute-start.1 = (bf16[128,7168]{1,0:T(8,128)(2,1)}, bf16[128,7168]{1,0:T(8,128)(2,1)}, u32[]{:S(2)}, u32[]{:S(2)}) collective-permute-start(bf16[128,7168]{1,0:T(8,128)(2,1)} %collective-permute-done), channel_id=1, source_target_pairs={{0,4},{4,8},{8,12},{12,0},{1,5},{5,9},{9,13},{13,1},{2,6},{6,10},{... | collective-permute-start | bytes 5505032 | tf_op jit(solution)/shard_map/ppermute | solution.py:33
  93.1 114.4 %collective-permute-start.4 = (bf16[128,7168]{1,0:T(8,128)(2,1)}, bf16[128,7168]{1,0:T(8,128)(2,1)}, u32[]{:S(2)}, u32[]{:S(2)}) collective-permute-start(bf16[128,7168]{1,0:T(8,128)(2,1)} %collective-permute-done.3), channel_id=1, source_target_pairs={{0,4},{4,8},{8,12},{12,0},{1,5},{5,9},{9,13},{13,1},{2,6},{6,10},{... | collective-permute-start | bytes 5505032 | tf_op jit(solution)/shard_map/ppermute | solution.py:33
  171.9 22.9 %copy-start.4 = (f32[1,128,2,2048]{3,1,2,0:T(8,128)S(1)}, f32[1,128,2,2048]{3,1,2,0:T(8,128)}, u32[]{:S(2)}) copy-start(f32[1,128,2,2048]{3,1,2,0:T(8,128)} %convolution_bitcast_fusion.6) | copy-start | bytes 6291460
  171.9 22.9 %copy-start.6 = (f32[1,128,2,2048]{3,1,2,0:T(8,128)S(1)}, f32[1,128,2,2048]{3,1,2,0:T(8,128)}, u32[]{:S(2)}) copy-start(f32[1,128,2,2048]{3,1,2,0:T(8,128)} %convolution_bitcast_fusion.4) | copy-start | bytes 6291460
  207.5 22.9 %copy-start.2 = (f32[1,128,2,2048]{3,1,2,0:T(8,128)S(1)}, f32[1,128,2,2048]{3,1,2,0:T(8,128)}, u32[]{:S(2)}) copy-start(f32[1,128,2,2048]{3,1,2,0:T(8,128)} %convolution_bitcast_fusion.1) | copy-start | bytes 6291460
  207.5 22.9 %copy-start.3 = (f32[1,128,2,2048]{3,1,2,0:T(8,128)S(1)}, f32[1,128,2,2048]{3,1,2,0:T(8,128)}, u32[]{:S(2)}) copy-start(f32[1,128,2,2048]{3,1,2,0:T(8,128)} %convolution_bitcast_fusion.2) | copy-start | bytes 6291460
  207.5 22.9 %copy-start.5 = (f32[1,128,2,2048]{3,1,2,0:T(8,128)S(1)}, f32[1,128,2,2048]{3,1,2,0:T(8,128)}, u32[]{:S(2)}) copy-start(f32[1,128,2,2048]{3,1,2,0:T(8,128)} %convolution_bitcast_fusion) | copy-start | bytes 6291460
  242.9 7.0 %copy-start = (f32[4,128,2,2048]{3,1,2,0:T(8,128)S(1)}, f32[4,128,2,2048]{3,1,2,0:T(8,128)}, u32[]{:S(2)}) copy-start(f32[4,128,2,2048]{3,1,2,0:T(8,128)} %gather_fusion.1) | copy-start | bytes 25165828
  242.9 8.2 %copy-start.1 = (f32[4,128,2048]{2,1,0:T(8,128)S(1)}, f32[4,128,2048]{2,1,0:T(8,128)}, u32[]{:S(2)}) copy-start(f32[4,128,2048]{2,1,0:T(8,128)} %convert.3) | copy-start | bytes 12582916
  251.1 34.8 %copy-start.7 = (f32[2,512]{1,0:T(2,128)S(1)}, f32[2,512]{1,0:T(2,128)}, u32[]{:S(2)}) copy-start(f32[2,512]{1,0:T(2,128)} %convert_divide_fusion) | copy-start | bytes 12292
Sparse Core Ops, SparseCore 0:
  9.0 48.3 all-gather.4
  59.0 44.4 all-gather.6
